TPU v7x, 32 devices: a whole 2x2x4 slice. The times are simulated.
32 devices in a mesh: oi: 4 (over y, x), oj: 8 (over z, core).
Axes of the slice: x: 2, y: 2, z: 4, core: 2. Of those that a mesh axis runs over, the one named last changes fastest.
Arguments:
- amplitudes: float32 [128, 128, 128], P(('oi', 'oj')), may hold values from -4 to 4
- integrals: float32 [128, 128, 128], P(('oi', 'oj')), may hold values from -6 to 6
- pno_energy: float32 [128, 128], P(('oi', 'oj')), may hold values from 0.3 to 3
- pair_shift: float32 [128], P(('oi', 'oj')), may hold values from 0.5 to 2
- column_margin: bfloat16 [4096, 128, 128], P(('oi', 'oj')), may hold values from -0.5 to 1.8, as said below
- row_margin: bfloat16 [4096, 128, 128], P(('oi', 'oj')), may hold values from -0.5 to 1.8, as said below
- column_coupling: float32 [4096], P(('oi', 'oj')), may hold values from -0.3 to 0.3
- row_coupling: float32 [4096], P(('oi', 'oj')), may hold values from -0.3 to 0.3
- column_target: int32 [4096], P(('oi', 'oj')), may hold values from 0 to 3
- row_target: int32 [4096], P(('oi', 'oj')), may hold values from 0 to 3
- column_source: int32 [4096], P(('oi', 'oj')), may hold values from 0 to 7
- row_source: int32 [4096], P(('oi', 'oj')), may hold values from 0 to 15
- column_sends: int32 [128, 2], P(('oi', 'oj')), may hold values from 0 to 3, as said below
- row_sends: int32 [256, 2], P(('oi', 'oj')), may hold values from 0 to 3, as said below
- term_counts: int32 [32, 2], P(('oi', 'oj')), may hold values from 1 to 128, as said below
Outputs:
- updated: float32 [128, 128, 128], P(('oi', 'oj'))
- residual: float32 [128, 128, 128], P(('oi', 'oj'))
Inputs may be any that keep to these rules, and one draw needn't show every extreme that they name: `column_margin`: each margin block is a 128 by 128 matrix of rank 128. `row_margin`: each margin block is a 128 by 128 matrix of rank 128. `column_sends`: each row names 2 different local pairs of its device. `row_sends`: each row names 2 different local pairs of its device. `term_counts`: some device has 128 live column terms and some device 128 live row terms.
All inputs are finite; a program needn't handle non-finite values.
Results may differ from a plain program's by a relative error of at most 0.0041.
Values may be sent and summed in bfloat16 or wider, within the bound.
A program may use at most 128 MiB of HBM per device.

v0:
```python
import functools

import jax
import jax.numpy as jnp
from jax import lax
from jax.experimental import pallas as pl
from jax.experimental.pallas import tpu as pltpu
from jax.sharding import PartitionSpec as P

ITERS = 2
CHUNK = 16
GROUP = 4
UNROLL = 4
AXES = ("oi", "oj")
MESH = pl.DeviceIdType.MESH


def partner(index, k, size):
    if size & (size - 1):
        return lax.rem(index + k, size)
    flipped = index
    bit = 1
    while bit < size:
        if k & bit:
            flipped = flipped + bit - 2 * bit * lax.rem(index // bit, 2)
        bit *= 2
    return flipped


def slot_count(terms, pairs):
    step = GROUP * UNROLL
    return -(-(terms + pairs * (GROUP - 1)) // step) * step


def arrange(coupling, target, source, live, pairs):
    terms = coupling.shape[0]
    slots = -(-slot_count(terms, pairs) // 128) * 128
    term_ids = jnp.arange(terms, dtype=jnp.int32)
    weight = jnp.where(term_ids < live, coupling, 0.0)
    same = (target[:, None] == target[None, :]) & (term_ids[:, None] > term_ids[None, :])
    rank = jnp.sum(same.astype(jnp.int32), axis=1)
    pair_ids = jnp.arange(pairs, dtype=jnp.int32)
    member = (target[:, None] == pair_ids[None, :]).astype(jnp.int32)
    groups = (jnp.sum(member, axis=0) + GROUP - 1) // GROUP
    before = jnp.sum(jnp.where(pair_ids[None, :] < pair_ids[:, None], groups[None, :], 0), axis=1)
    base = jnp.sum(member * before[None, :], axis=1) * GROUP
    slot = base + rank
    slot_ids = jnp.arange(slots, dtype=jnp.int32)
    hot = slot[None, :] == slot_ids[:, None]

    def place(values):
        return jnp.sum(jnp.where(hot, values[None, :], jnp.zeros_like(values)[None, :]), axis=1)

    return place(weight), place(term_ids), place(source), place(target)


def jacobi_kernel(
    sizes,
    amplitudes_hbm,
    integrals_hbm,
    pno_energy_hbm,
    pair_shift_hbm,
    column_margin,
    row_margin,
    weights_hbm,
    orders_hbm,
    sources_hbm,
    targets_hbm,
    column_sends_hbm,
    row_sends_hbm,
    latest_hbm,
    total_hbm,
    amplitudes,
    integrals,
    pno_energy,
    pair_shift,
    weights,
    orders,
    sources,
    targets,
    column_sends,
    row_sends,
    margins,
    total,
    frozen,
    column_out,
    row_out,
    column_first,
    row_first,
    column_later,
    row_later,
    input_sems,
    margin_sems,
    column_send_sems,
    column_recv_sems,
    row_send_sems,
    row_recv_sems,
    output_sems,
):
    pairs, width = pno_energy.shape
    terms = margins.shape[1]
    cap = column_out.shape[2]
    chunks = terms // CHUNK
    me = [lax.axis_index(axis) for axis in AXES]
    margin_refs = (column_margin, row_margin)
    sends = (column_sends, row_sends)
    outs = (column_out, row_out)
    ins = ((column_first, row_first), (column_later, row_later))
    send_sems = (column_send_sems, row_send_sems)
    recv_sems = (column_recv_sems, row_recv_sems)

    staged = (
        (column_sends_hbm, column_sends),
        (row_sends_hbm, row_sends),
        (amplitudes_hbm, amplitudes),
        (weights_hbm, weights),
        (orders_hbm, orders),
        (sources_hbm, sources),
        (targets_hbm, targets),
        (pair_shift_hbm, pair_shift),
        (pno_energy_hbm, pno_energy),
        (integrals_hbm, integrals),
    )
    stage_copies = [
        pltpu.make_async_copy(source, target, input_sems.at[i])
        for i, (source, target) in enumerate(staged)
    ]
    for copy in stage_copies:
        copy.start()

    barrier = pltpu.get_barrier_semaphore()
    for side in range(2):
        for k in range(1, sizes[side]):
            peer = partner(me[side], k, sizes[side])
            pl.semaphore_signal(
                barrier, inc=1, device_id={AXES[side]: peer}, device_id_type=MESH
            )

    def fetch(side, chunk):
        part = pl.ds(chunk * CHUNK, CHUNK)
        return pltpu.make_async_copy(
            margin_refs[side].at[part], margins.at[side, part], margin_sems.at[side, chunk]
        )

    for side in range(2):
        for chunk in range(chunks):
            fetch(side, chunk).start()

    for copy in stage_copies[:3]:
        copy.wait()
    for p in range(pairs):
        frozen[p] = amplitudes[p].astype(jnp.bfloat16)

    def exchange(sweep, side, k):
        peer = partner(me[side], k, sizes[side])
        return pltpu.make_async_remote_copy(
            src_ref=outs[side].at[sweep, k],
            dst_ref=ins[sweep][side].at[pl.ds(me[side] * cap, cap)],
            send_sem=send_sems[side].at[sweep, k],
            recv_sem=recv_sems[side].at[sweep, k],
            device_id={AXES[side]: peer},
            device_id_type=MESH,
        )

    def pack(sweep, side):
        for k in range(sizes[side]):
            peer = partner(me[side], k, sizes[side])
            for c in range(cap):
                block = frozen[sends[side][c, peer]]
                if k == 0:
                    ins[sweep][side][me[side] * cap + c] = block
                else:
                    outs[side][sweep, k, c] = block

    def launch(sweep):
        for side in (1, 0):
            pack(sweep, side)
            if sweep == 0 and side == 1:
                pl.semaphore_wait(barrier, sizes[0] + sizes[1] - 2)
            for k in reversed(range(1, sizes[side])):
                exchange(sweep, side, k).start()

    slots = slot_count(terms, pairs)

    def couple(sweep, side):
        blocks = ins[sweep][side]

        def step(index, carry):
            for u in range(UNROLL):
                first = (index * UNROLL + u) * GROUP
                slot = [first + i for i in range(GROUP)]
                margin = [margins[side, orders[side, i]] for i in slot]
                block = [blocks[sources[side, i]] for i in slot]
                halves = []
                for i in range(0, GROUP, 2):
                    empty = jnp.zeros_like(block[i])
                    both = jnp.concatenate(
                        [
                            jnp.concatenate([block[i], empty], axis=1),
                            jnp.concatenate([empty, block[i + 1]], axis=1),
                        ],
                        axis=0,
                    )
                    half = jnp.dot(
                        jnp.concatenate(margin[i : i + 2], axis=1),
                        both,
                        preferred_element_type=jnp.float32,
                    )
                    for j in range(2):
                        part = half[:, j * width : (j + 1) * width]
                        halves.append((part * weights[side, slot[i + j]]).astype(jnp.bfloat16))
                whole = lax.dot_general(
                    jnp.concatenate(halves, axis=1),
                    jnp.concatenate(margin, axis=1),
                    (((1,), (1,)), ((), ())),
                    preferred_element_type=jnp.float32,
                )
                target = targets[side, first]
                for p in range(pairs):
                    total[p] += whole * jnp.where(target == p, 1.0, 0.0)
            return carry

        lax.fori_loop(0, slots // (GROUP * UNROLL), step, 0)

    for sweep in range(ITERS):
        launch(sweep)
        total[...] = jnp.zeros_like(total)
        if sweep == 0:
            for copy in stage_copies[3:]:
                copy.wait()
            for side in range(2):
                for chunk in range(chunks):
                    fetch(side, chunk).wait()
        for side in range(2):
            for k in range(1, sizes[side]):
                exchange(sweep, side, k).wait_recv()
            couple(sweep, side)
        for p in range(pairs if sweep < ITERS - 1 else 0):
            across = jnp.broadcast_to(pno_energy[p : p + 1, :], (width, width))
            divisor = across.T + across + pair_shift[p]
            old = amplitudes[p]
            rest = integrals[p] + divisor * old + total[p]
            new = old - rest / divisor
            frozen[p] = new.astype(jnp.bfloat16)
            amplitudes[p] = new

    results = (
        pltpu.make_async_copy(amplitudes, latest_hbm, output_sems.at[0]),
        pltpu.make_async_copy(total, total_hbm, output_sems.at[1]),
    )
    for copy in results:
        copy.start()
    for sweep in range(ITERS):
        for side in range(2):
            for k in range(1, sizes[side]):
                exchange(sweep, side, k).wait_send()
    for copy in results:
        copy.wait()


def shards(sizes, *operands):
    counts = operands[14]
    pairs = operands[0].shape[0]
    couplings, targets, sources = (jnp.stack(operands[i : i + 2]) for i in (6, 8, 10))
    arranged = jax.vmap(functools.partial(arrange, pairs=pairs))(
        couplings, targets, sources, counts[0]
    )
    operands = operands[:6] + arranged + (operands[12].T, operands[13].T)
    amplitudes, pno_energy, column_margin = operands[0], operands[2], operands[4]
    column_sends = operands[10]
    terms, width, _ = column_margin.shape
    cap = column_sends.shape[0]
    hbm = pl.BlockSpec(memory_space=pltpu.HBM)
    in_vmem = (0, 1, 2)
    in_smem = (3,) + tuple(range(6, 12))

    def held(i, space):
        return space(operands[i].shape, operands[i].dtype)

    def buffer(*shape):
        return pltpu.VMEM(shape + (width, width), jnp.bfloat16)

    dma = pltpu.SemaphoreType.DMA
    latest, coupled = pl.pallas_call(
            functools.partial(jacobi_kernel, sizes),
            out_shape=[jax.ShapeDtypeStruct(amplitudes.shape, jnp.float32)] * 2,
            in_specs=[hbm] * len(operands),
            out_specs=[hbm] * 2,
            scratch_shapes=[held(i, pltpu.VMEM) for i in in_vmem]
            + [held(i, pltpu.SMEM) for i in in_smem]
            + [
                buffer(2, terms),
                pltpu.VMEM(amplitudes.shape, jnp.float32),
                buffer(amplitudes.shape[0]),
                buffer(ITERS, sizes[0], cap),
                buffer(ITERS, sizes[1], cap),
            ]
            + [buffer(size * cap) for size in sizes] * ITERS
            + [
                dma((len(in_vmem) + len(in_smem),)),
                dma((2, terms // CHUNK)),
                dma((ITERS, sizes[0])),
                dma((ITERS, sizes[0])),
                dma((ITERS, sizes[1])),
                dma((ITERS, sizes[1])),
                dma((2,)),
            ],
            compiler_params=pltpu.CompilerParams(
                collective_id=0,
                has_side_effects=True,
            ),
            name="jacobi",
        )(*operands)
    integrals, pair_shift = operands[1], operands[3]
    divisor = pno_energy[:, :, None] + pno_energy[:, None, :] + pair_shift[:, None, None]
    residual = integrals + divisor * latest + coupled
    return (latest - residual / divisor, residual)


def solution(mesh):
    sizes = tuple(mesh.shape[axis] for axis in AXES)
    in_specs = (
        (P(AXES, None, None),) * 2
        + (P(AXES, None), P(AXES))
        + (P(AXES, None, None),) * 2
        + (P(AXES),) * 6
        + (P(AXES, None),) * 3
    )
    out_specs = (P(AXES, None, None), P(AXES, None, None))
    return jax.shard_map(
        functools.partial(shards, sizes),
        mesh=mesh,
        in_specs=in_specs,
        out_specs=out_specs,
        check_vma=False,
    )
```

profile of v0, /device:TPU:0, one launch (start us, length us, event | category | flops | bytes accessed | tf_op | source)
XLA Modules:
  0.0 46.3 jit_solution(211269062249543397)
XLA Ops:
  0.6 0.8 %compare_select_fusion = f32[2,128]{1,0:T(2,128)S(1)} fusion(f32[1,128]{1,0:T(1,128)} %bitcast.11, f32[1,128]{1,0:T(1,128)} %bitcast.12, s32[2]{0:T(128)} %bitcast.13), kind=kLoop, calls=%fused_computation.15 | loop fusion | flops 768 | bytes 2056 | tf_op jit(solution)/shard_map/vmap(jit(_where))/select_n | solution.py:39
  1.4 0.7 %pad_add_fusion = (s32[2,128]{1,0:T(2,128)S(1)}, s32[2,128]{1,0:T(2,128)S(1)}) fusion(s32[1,128]{1,0:T(1,128)} %bitcast.14, s32[1,128]{1,0:T(1,128)} %bitcast.15, s32[1,128]{1,0:T(1,128)} %bitcast.16, s32[1,128]{1,0:T(1,128)} %bitcast.17), kind=kLoop, calls=%fused_computation.20 | loop fusion | flops 512 | bytes 4096 | tf_op jit(solution)/shard_map/stack | solution.py:264
  2.1 0.1 convert_reduce_fusion.1
  2.3 0.2 select_reduce_fusion.5
  2.4 0.1 select_reduce_fusion.4
  2.5 0.2 convert_reduce_fusion
  2.7 0.7 %select_reduce_fusion.3.weights_hbm = f32[2,256]{1,0:T(2,128)} fusion(f32[2,128]{1,0:T(2,128)S(1)} %compare_select_fusion, s32[2,128]{1,0:T(2,128)S(1)} %multiply_add_fusion), kind=kLoop, calls=%fused_computation.6 | loop fusion | flops 196096 | bytes 4096 | tf_op jit(solution)/shard_map/vmap()/reduce_sum | solution.py:52
  3.5 0.9 %select_reduce_fusion = (s32[2,256]{1,0:T(2,128)}, s32[2,256]{1,0:T(2,128)}, s32[2,256]{1,0:T(2,128)}) fusion(s32[2,128]{1,0:T(2,128)S(1)} %get-tuple-element.11, s32[2,128]{1,0:T(2,128)S(1)} %multiply_add_fusion, s32[2,128]{1,0:T(2,128)S(1)} %get-tuple-element.12), kind=kLoop, calls=%fused_computation.3 | loop fusion | flops 457216 | bytes 9216 | tf_op jit(solution)/shard_map/vmap()/reduce_sum | solution.py:52
  4.3 0.0 copy-start
  4.3 0.0 copy-start.1
  4.3 0.0 copy-start.2
  4.3 40.0 %jacobi.1 = (f32[4,128,128]{2,1,0:T(8,128)}, f32[4,128,128]{2,1,0:T(8,128)}) custom-call(f32[4,128,128]{2,1,0:T(8,128)} %amplitudes_hbm.1, f32[4,128,128]{2,1,0:T(8,128)} %integrals_hbm.1, f32[4,128]{1,0:T(4,128)} %pno_energy_hbm.1, f32[4]{0:T(128)} %pair_shift_hbm.1, bf16[128,128,128]{2,1,0:T(8,128)(2,1)} %column_margin.1, ...), custom_call_target="tpu_custom_call" | custom-call | tf_op jit(solution)/shard_map/jacobi/pallas_call | solution.py:284
  44.3 0.0 copy-done
  44.3 0.0 copy-done.1
  44.3 0.0 copy-done.2
  44.4 2.0 %divide_subtract_fusion = (f32[4,128,128]{2,1,0:T(8,128)}, f32[4,128,128]{2,1,0:T(8,128)}) fusion(f32[4,128,128]{2,1,0:T(8,128)} %get-tuple-element.4, f32[4]{0:T(128)S(1)} %copy-done.2, f32[4,128]{1,0:T(4,128)S(1)} %copy-done.1, f32[4,128,128]{2,1,0:T(8,128)} %get-tuple-element.5, f32[4,128,128]{2,1,0:T(8,128)S(1)} %copy-done), kind=kLoop, calls=%fused_computation | loop fusion | flops 458752 | bytes 1312784 | tf_op jit(solution)/shard_map/sub | solution.py:317
  (4 shorter events, 0.0 us)
Async XLA Ops:
  4.3 40.0 %copy-start = (f32[4,128,128]{2,1,0:T(8,128)S(1)}, f32[4,128,128]{2,1,0:T(8,128)}, u32[]{:S(2)}) copy-start(f32[4,128,128]{2,1,0:T(8,128)} %integrals_hbm.1) | copy-start | bytes 786436
  4.3 40.0 %copy-start.1 = (f32[4,128]{1,0:T(4,128)S(1)}, f32[4,128]{1,0:T(4,128)}, u32[]{:S(2)}) copy-start(f32[4,128]{1,0:T(4,128)} %pno_energy_hbm.1) | copy-start | bytes 6148
  4.3 40.0 %copy-start.2 = (f32[4]{0:T(128)S(1)}, f32[4]{0:T(128)}, u32[]{:S(2)}) copy-start(f32[4]{0:T(128)} %pair_shift_hbm.1) | copy-start | bytes 52
where the time goes:
time: 46.5 us; the launch traced here: 46.3 us
  Pallas kernels  40 us (86%)
  other arithmetic  5.65 us (12%)
  between operations  0.69 us (1%)
    pallas_call x1, Pallas kernels, shards(): pl.pallas_call(functools.partial(jacobi_kernel, sizes), out_shape=[jax.Sh...  40 us
    sub x1, other arithmetic, shards(): return (latest - residual / divisor, residual)  1.97 us
    reduce_sum x2, other arithmetic, place(): jnp.sum(jnp.where(hot, values[None, :], jnp.zeros_like(values)[None, :]),...  1.61 us

commit v1 on v0

--- a/solution.py
+++ b/solution.py
@@ -10,7 +10,7 @@
 ITERS = 2
 CHUNK = 16
 GROUP = 4
-UNROLL = 4
+UNROLL = 18
 AXES = ("oi", "oj")
 MESH = pl.DeviceIdType.MESH
 

time: 46.5 us -> 42.7 us (0.918)
  Pallas kernels: 40 us -> 36.2 us
    pallas_call x1, Pallas kernels: 40 us -> 36.2 us  [shards(): pl.pallas_call(functools.partial(jacobi_kernel, sizes), out_shape=[jax.Sh...]
where the time goes in v1:
time: 42.7 us; the launch traced here: 42.5 us
  Pallas kernels  36.2 us (85%)
  other arithmetic  5.65 us (13%)
  between operations  0.69 us (2%)
    pallas_call x1, Pallas kernels, shards(): pl.pallas_call(functools.partial(jacobi_kernel, sizes), out_shape=[jax.Sh...  36.2 us
    sub x1, other arithmetic, shards(): return (latest - residual / divisor, residual)  1.97 us
    reduce_sum x2, other arithmetic, place(): jnp.sum(jnp.where(hot, values[None, :], jnp.zeros_like(values)[None, :]),...  1.61 us

profile of v1, /device:TPU:0, one launch (start us, length us, event | category | flops | bytes accessed | tf_op | source)
XLA Modules:
  0.0 42.5 jit_solution(12648092888914375820)
XLA Ops:
  0.6 0.8 %compare_select_fusion = f32[2,128]{1,0:T(2,128)S(1)} fusion(f32[1,128]{1,0:T(1,128)} %bitcast.11, f32[1,128]{1,0:T(1,128)} %bitcast.12, s32[2]{0:T(128)} %bitcast.13), kind=kLoop, calls=%fused_computation.15 | loop fusion | flops 768 | bytes 2056 | tf_op jit(solution)/shard_map/vmap(jit(_where))/select_n | solution.py:39
  1.4 0.7 %pad_add_fusion = (s32[2,128]{1,0:T(2,128)S(1)}, s32[2,128]{1,0:T(2,128)S(1)}) fusion(s32[1,128]{1,0:T(1,128)} %bitcast.14, s32[1,128]{1,0:T(1,128)} %bitcast.15, s32[1,128]{1,0:T(1,128)} %bitcast.16, s32[1,128]{1,0:T(1,128)} %bitcast.17), kind=kLoop, calls=%fused_computation.20 | loop fusion | flops 512 | bytes 4096 | tf_op jit(solution)/shard_map/stack | solution.py:264
  2.1 0.1 convert_reduce_fusion.1
  2.3 0.2 select_reduce_fusion.5
  2.4 0.1 select_reduce_fusion.4
  2.5 0.2 convert_reduce_fusion
  2.7 0.7 %select_reduce_fusion.3.weights_hbm = f32[2,256]{1,0:T(2,128)} fusion(f32[2,128]{1,0:T(2,128)S(1)} %compare_select_fusion, s32[2,128]{1,0:T(2,128)S(1)} %multiply_add_fusion), kind=kLoop, calls=%fused_computation.6 | loop fusion | flops 196096 | bytes 4096 | tf_op jit(solution)/shard_map/vmap()/reduce_sum | solution.py:52
  3.5 0.9 %select_reduce_fusion = (s32[2,256]{1,0:T(2,128)}, s32[2,256]{1,0:T(2,128)}, s32[2,256]{1,0:T(2,128)}) fusion(s32[2,128]{1,0:T(2,128)S(1)} %get-tuple-element.11, s32[2,128]{1,0:T(2,128)S(1)} %multiply_add_fusion, s32[2,128]{1,0:T(2,128)S(1)} %get-tuple-element.12), kind=kLoop, calls=%fused_computation.3 | loop fusion | flops 457216 | bytes 9216 | tf_op jit(solution)/shard_map/vmap()/reduce_sum | solution.py:52
  4.3 0.0 copy-start
  4.3 0.0 copy-start.1
  4.3 0.0 copy-start.2
  4.3 36.2 %jacobi.1 = (f32[4,128,128]{2,1,0:T(8,128)}, f32[4,128,128]{2,1,0:T(8,128)}) custom-call(f32[4,128,128]{2,1,0:T(8,128)} %amplitudes_hbm.1, f32[4,128,128]{2,1,0:T(8,128)} %integrals_hbm.1, f32[4,128]{1,0:T(4,128)} %pno_energy_hbm.1, f32[4]{0:T(128)} %pair_shift_hbm.1, bf16[128,128,128]{2,1,0:T(8,128)(2,1)} %column_margin.1, ...), custom_call_target="tpu_custom_call" | custom-call | tf_op jit(solution)/shard_map/jacobi/pallas_call | solution.py:284
  40.5 0.0 copy-done
  40.5 0.0 copy-done.1
  40.5 0.0 copy-done.2
  40.5 2.0 %divide_subtract_fusion = (f32[4,128,128]{2,1,0:T(8,128)}, f32[4,128,128]{2,1,0:T(8,128)}) fusion(f32[4,128,128]{2,1,0:T(8,128)} %get-tuple-element.4, f32[4]{0:T(128)S(1)} %copy-done.2, f32[4,128]{1,0:T(4,128)S(1)} %copy-done.1, f32[4,128,128]{2,1,0:T(8,128)} %get-tuple-element.5, f32[4,128,128]{2,1,0:T(8,128)S(1)} %copy-done), kind=kLoop, calls=%fused_computation | loop fusion | flops 458752 | bytes 1312784 | tf_op jit(solution)/shard_map/sub | solution.py:317
  (4 shorter events, 0.0 us)
Async XLA Ops:
  4.3 36.2 %copy-start = (f32[4,128,128]{2,1,0:T(8,128)S(1)}, f32[4,128,128]{2,1,0:T(8,128)}, u32[]{:S(2)}) copy-start(f32[4,128,128]{2,1,0:T(8,128)} %integrals_hbm.1) | copy-start | bytes 786436
  4.3 36.2 %copy-start.1 = (f32[4,128]{1,0:T(4,128)S(1)}, f32[4,128]{1,0:T(4,128)}, u32[]{:S(2)}) copy-start(f32[4,128]{1,0:T(4,128)} %pno_energy_hbm.1) | copy-start | bytes 6148
  4.3 36.2 %copy-start.2 = (f32[4]{0:T(128)S(1)}, f32[4]{0:T(128)}, u32[]{:S(2)}) copy-start(f32[4]{0:T(128)} %pair_shift_hbm.1) | copy-start | bytes 52

commit v2 on v1

--- a/solution.py
+++ b/solution.py
@@ -25,6 +25,10 @@
             flipped = flipped + bit - 2 * bit * lax.rem(index // bit, 2)
         bit *= 2
     return flipped
+
+
+def relayed(size):
+    return size >= 8 and not size & (size - 1)
 
 
 def slot_count(terms, pairs):
@@ -89,12 +93,18 @@
     row_first,
     column_later,
     row_later,
+    whole_first,
+    whole_later,
+    table_in,
+    table,
     input_sems,
     margin_sems,
     column_send_sems,
     column_recv_sems,
     row_send_sems,
     row_recv_sems,
+    whole_sems,
+    table_sems,
     output_sems,
 ):
     pairs, width = pno_energy.shape
@@ -149,7 +159,46 @@
     for copy in stage_copies[:3]:
         copy.wait()
     for p in range(pairs):
-        frozen[p] = amplitudes[p].astype(jnp.bfloat16)
+        frozen[0, p] = amplitudes[p].astype(jnp.bfloat16)
+
+    count = sizes[1]
+    relay = relayed(count)
+    whole_in = (whole_first, whole_later)
+    chip = me[1] // 2
+    inner = (chip == count // 4 - 1) | (chip == count // 4)
+    opposite = partner(me[1], count - 2, count)
+    handed = (count - 4, count - 3, count - 1) if relay else ()
+
+    def send_whole(sweep):
+        return pltpu.make_async_remote_copy(
+            src_ref=frozen.at[sweep],
+            dst_ref=whole_in[sweep],
+            send_sem=whole_sems.at[0, sweep],
+            recv_sem=whole_sems.at[1, sweep],
+            device_id={AXES[1]: opposite},
+            device_id_type=MESH,
+        )
+
+    def send_table():
+        return pltpu.make_async_remote_copy(
+            src_ref=row_sends_hbm,
+            dst_ref=table_in,
+            send_sem=table_sems.at[0],
+            recv_sem=table_sems.at[1],
+            device_id={AXES[1]: opposite},
+            device_id_type=MESH,
+        )
+
+    def hand_on(sweep, k):
+        peer = partner(opposite, k, count)
+        return pltpu.make_async_remote_copy(
+            src_ref=outs[1].at[sweep, k],
+            dst_ref=ins[sweep][1].at[pl.ds(opposite * cap, cap)],
+            send_sem=send_sems[1].at[sweep, k],
+            recv_sem=recv_sems[1].at[sweep, k],
+            device_id={AXES[1]: peer},
+            device_id_type=MESH,
+        )
 
     def exchange(sweep, side, k):
         peer = partner(me[side], k, sizes[side])
@@ -162,23 +211,96 @@
             device_id_type=MESH,
         )
 
-    def pack(sweep, side):
-        for k in range(sizes[side]):
-            peer = partner(me[side], k, sizes[side])
-            for c in range(cap):
-                block = frozen[sends[side][c, peer]]
-                if k == 0:
-                    ins[sweep][side][me[side] * cap + c] = block
-                else:
-                    outs[side][sweep, k, c] = block
+    def pack(sweep, side, k):
+        peer = partner(me[side], k, sizes[side])
+        for c in range(cap):
+            block = frozen[sweep, sends[side][c, peer]]
+            if k == 0:
+                ins[sweep][side][me[side] * cap + c] = block
+            else:
+                outs[side][sweep, k, c] = block
+
+    def send(sweep, side, k):
+        pack(sweep, side, k)
+        exchange(sweep, side, k).start()
 
     def launch(sweep):
-        for side in (1, 0):
-            pack(sweep, side)
-            if sweep == 0 and side == 1:
-                pl.semaphore_wait(barrier, sizes[0] + sizes[1] - 2)
-            for k in reversed(range(1, sizes[side])):
-                exchange(sweep, side, k).start()
+        if sweep == 0:
+            pl.semaphore_wait(barrier, sizes[0] + sizes[1] - 2)
+        if relay:
+
+            @pl.when(inner)
+            def _():
+                send_whole(sweep).start()
+                if sweep == 0:
+                    send_table().start()
+
+        near = [k for k in (2, 3) if k < count]
+        for k in near:
+            send(sweep, 1, k)
+        far = [k for k in reversed(range(4, count)) if not relay or k < count - 4]
+        for k in far:
+            send(sweep, 1, k)
+        if relay:
+
+            @pl.when(jnp.logical_not(inner))
+            def _():
+                for k in (count - 2, count - 1, count - 4, count - 3):
+                    send(sweep, 1, k)
+
+        if count > 1:
+            send(sweep, 1, 1)
+        for k in reversed(range(1, sizes[0])):
+            send(sweep, 0, k)
+        for side in range(2):
+            pack(sweep, side, 0)
+
+    def pass_on(sweep):
+        if relay:
+
+            @pl.when(inner)
+            def _():
+                if sweep == 0:
+                    send_table().wait_recv()
+                    lookup = pltpu.make_async_copy(table_in, table, table_sems.at[2])
+                    lookup.start()
+                    lookup.wait()
+                send_whole(sweep).wait_recv()
+                for k in handed:
+                    peer = partner(opposite, k, count)
+                    for c in range(cap):
+                        outs[1][sweep, k, c] = whole_in[sweep][table[c, peer]]
+                    hand_on(sweep, k).start()
+                for c in range(cap):
+                    ins[sweep][1][opposite * cap + c] = whole_in[sweep][table[c, me[1]]]
+
+    def received(sweep, side):
+        for k in range(1, sizes[side]):
+            if side == 1 and relay and k == count - 2:
+
+                @pl.when(jnp.logical_not(inner))
+                def _():
+                    exchange(sweep, side, k).wait_recv()
+
+            else:
+                exchange(sweep, side, k).wait_recv()
+
+    def sent(sweep, side):
+        for k in range(1, sizes[side]):
+            if side == 1 and relay and k == count - 2:
+
+                @pl.when(jnp.logical_not(inner))
+                def _():
+                    exchange(sweep, side, k).wait_send()
+
+                @pl.when(inner)
+                def _():
+                    send_whole(sweep).wait_send()
+                    if sweep == 0:
+                        send_table().wait_send()
+
+            else:
+                exchange(sweep, side, k).wait_send()
 
     slots = slot_count(terms, pairs)
 
@@ -224,6 +346,7 @@
 
     for sweep in range(ITERS):
         launch(sweep)
+        pass_on(sweep)
         total[...] = jnp.zeros_like(total)
         if sweep == 0:
             for copy in stage_copies[3:]:
@@ -232,8 +355,7 @@
                 for chunk in range(chunks):
                     fetch(side, chunk).wait()
         for side in range(2):
-            for k in range(1, sizes[side]):
-                exchange(sweep, side, k).wait_recv()
+            received(sweep, side)
             couple(sweep, side)
         for p in range(pairs if sweep < ITERS - 1 else 0):
             across = jnp.broadcast_to(pno_energy[p : p + 1, :], (width, width))
@@ -241,7 +363,7 @@
             old = amplitudes[p]
             rest = integrals[p] + divisor * old + total[p]
             new = old - rest / divisor
-            frozen[p] = new.astype(jnp.bfloat16)
+            frozen[sweep + 1, p] = new.astype(jnp.bfloat16)
             amplitudes[p] = new
 
     results = (
@@ -252,8 +374,7 @@
         copy.start()
     for sweep in range(ITERS):
         for side in range(2):
-            for k in range(1, sizes[side]):
-                exchange(sweep, side, k).wait_send()
+            sent(sweep, side)
     for copy in results:
         copy.wait()
 
@@ -291,11 +412,16 @@
             + [
                 buffer(2, terms),
                 pltpu.VMEM(amplitudes.shape, jnp.float32),
-                buffer(amplitudes.shape[0]),
+                buffer(ITERS, amplitudes.shape[0]),
                 buffer(ITERS, sizes[0], cap),
                 buffer(ITERS, sizes[1], cap),
             ]
             + [buffer(size * cap) for size in sizes] * ITERS
+            + [buffer(amplitudes.shape[0])] * ITERS
+            + [
+                held(11, pltpu.VMEM),
+                held(11, pltpu.SMEM),
+            ]
             + [
                 dma((len(in_vmem) + len(in_smem),)),
                 dma((2, terms // CHUNK)),
@@ -303,6 +429,8 @@
                 dma((ITERS, sizes[0])),
                 dma((ITERS, sizes[1])),
                 dma((ITERS, sizes[1])),
+                dma((2, ITERS)),
+                dma((3,)),
                 dma((2,)),
             ],
             compiler_params=pltpu.CompilerParams(

time: 42.7 us -> 41.3 us (0.967)
  Pallas kernels: 36.2 us -> 34.8 us
    pallas_call x1, Pallas kernels: 36.2 us -> 34.8 us  [shards(): pl.pallas_call(functools.partial(jacobi_kernel, sizes), out_shape=[jax.Sh...]
where the time goes in v2:
time: 41.3 us; the launch traced here: 41.2 us
  Pallas kernels  34.8 us (84%)
  other arithmetic  5.65 us (14%)
  between operations  0.69 us (2%)
    pallas_call x1, Pallas kernels, shards(): pl.pallas_call(functools.partial(jacobi_kernel, sizes), out_shape=[jax.Sh...  34.8 us
    sub x1, other arithmetic, shards(): return (latest - residual / divisor, residual)  1.97 us
    reduce_sum x2, other arithmetic, place(): jnp.sum(jnp.where(hot, values[None, :], jnp.zeros_like(values)[None, :]),...  1.61 us

profile of v2, /device:TPU:0, one launch (start us, length us, event | category | flops | bytes accessed | tf_op | source)
XLA Modules:
  0.0 41.2 jit_solution(2477271081767608102)
XLA Ops:
  0.6 0.8 %compare_select_fusion = f32[2,128]{1,0:T(2,128)S(1)} fusion(f32[1,128]{1,0:T(1,128)} %bitcast.11, f32[1,128]{1,0:T(1,128)} %bitcast.12, s32[2]{0:T(128)} %bitcast.13), kind=kLoop, calls=%fused_computation.15 | loop fusion | flops 768 | bytes 2056 | tf_op jit(solution)/shard_map/vmap(jit(_where))/select_n | solution.py:43
  1.4 0.7 %pad_add_fusion = (s32[2,128]{1,0:T(2,128)S(1)}, s32[2,128]{1,0:T(2,128)S(1)}) fusion(s32[1,128]{1,0:T(1,128)} %bitcast.14, s32[1,128]{1,0:T(1,128)} %bitcast.15, s32[1,128]{1,0:T(1,128)} %bitcast.16, s32[1,128]{1,0:T(1,128)} %bitcast.17), kind=kLoop, calls=%fused_computation.20 | loop fusion | flops 512 | bytes 4096 | tf_op jit(solution)/shard_map/stack | solution.py:385
  2.1 0.1 convert_reduce_fusion.1
  2.3 0.2 select_reduce_fusion.5
  2.4 0.1 select_reduce_fusion.4
  2.5 0.2 convert_reduce_fusion
  2.7 0.7 %select_reduce_fusion.3.weights_hbm = f32[2,256]{1,0:T(2,128)} fusion(f32[2,128]{1,0:T(2,128)S(1)} %compare_select_fusion, s32[2,128]{1,0:T(2,128)S(1)} %multiply_add_fusion), kind=kLoop, calls=%fused_computation.6 | loop fusion | flops 196096 | bytes 4096 | tf_op jit(solution)/shard_map/vmap()/reduce_sum | solution.py:56
  3.5 0.9 %select_reduce_fusion = (s32[2,256]{1,0:T(2,128)}, s32[2,256]{1,0:T(2,128)}, s32[2,256]{1,0:T(2,128)}) fusion(s32[2,128]{1,0:T(2,128)S(1)} %get-tuple-element.11, s32[2,128]{1,0:T(2,128)S(1)} %multiply_add_fusion, s32[2,128]{1,0:T(2,128)S(1)} %get-tuple-element.12), kind=kLoop, calls=%fused_computation.3 | loop fusion | flops 457216 | bytes 9216 | tf_op jit(solution)/shard_map/vmap()/reduce_sum | solution.py:56
  4.3 0.0 copy-start
  4.3 0.0 copy-start.1
  4.3 0.0 copy-start.2
  4.3 34.8 %jacobi.1 = (f32[4,128,128]{2,1,0:T(8,128)}, f32[4,128,128]{2,1,0:T(8,128)}) custom-call(f32[4,128,128]{2,1,0:T(8,128)} %amplitudes_hbm.1, f32[4,128,128]{2,1,0:T(8,128)} %integrals_hbm.1, f32[4,128]{1,0:T(4,128)} %pno_energy_hbm.1, f32[4]{0:T(128)} %pair_shift_hbm.1, bf16[128,128,128]{2,1,0:T(8,128)(2,1)} %column_margin.1, ...), custom_call_target="tpu_custom_call" | custom-call | tf_op jit(solution)/shard_map/jacobi/pallas_call | solution.py:405
  39.2 0.0 copy-done
  39.2 0.0 copy-done.1
  39.2 0.0 copy-done.2
  39.2 2.0 %divide_subtract_fusion = (f32[4,128,128]{2,1,0:T(8,128)}, f32[4,128,128]{2,1,0:T(8,128)}) fusion(f32[4,128,128]{2,1,0:T(8,128)} %get-tuple-element.4, f32[4]{0:T(128)S(1)} %copy-done.2, f32[4,128]{1,0:T(4,128)S(1)} %copy-done.1, f32[4,128,128]{2,1,0:T(8,128)} %get-tuple-element.5, f32[4,128,128]{2,1,0:T(8,128)S(1)} %copy-done), kind=kLoop, calls=%fused_computation | loop fusion | flops 458752 | bytes 1312784 | tf_op jit(solution)/shard_map/sub | solution.py:445
  (4 shorter events, 0.0 us)
Async XLA Ops:
  4.3 34.8 %copy-start = (f32[4,128,128]{2,1,0:T(8,128)S(1)}, f32[4,128,128]{2,1,0:T(8,128)}, u32[]{:S(2)}) copy-start(f32[4,128,128]{2,1,0:T(8,128)} %integrals_hbm.1) | copy-start | bytes 786436
  4.3 34.8 %copy-start.1 = (f32[4,128]{1,0:T(4,128)S(1)}, f32[4,128]{1,0:T(4,128)}, u32[]{:S(2)}) copy-start(f32[4,128]{1,0:T(4,128)} %pno_energy_hbm.1) | copy-start | bytes 6148
  4.3 34.9 %copy-start.2 = (f32[4]{0:T(128)S(1)}, f32[4]{0:T(128)}, u32[]{:S(2)}) copy-start(f32[4]{0:T(128)} %pair_shift_hbm.1) | copy-start | bytes 52

commit v3 on v2

--- a/solution.py
+++ b/solution.py
@@ -36,26 +36,34 @@
     return -(-(terms + pairs * (GROUP - 1)) // step) * step
 
 
-def arrange(coupling, target, source, live, pairs):
-    terms = coupling.shape[0]
-    slots = -(-slot_count(terms, pairs) // 128) * 128
-    term_ids = jnp.arange(terms, dtype=jnp.int32)
-    weight = jnp.where(term_ids < live, coupling, 0.0)
-    same = (target[:, None] == target[None, :]) & (term_ids[:, None] > term_ids[None, :])
-    rank = jnp.sum(same.astype(jnp.int32), axis=1)
-    pair_ids = jnp.arange(pairs, dtype=jnp.int32)
-    member = (target[:, None] == pair_ids[None, :]).astype(jnp.int32)
-    groups = (jnp.sum(member, axis=0) + GROUP - 1) // GROUP
-    before = jnp.sum(jnp.where(pair_ids[None, :] < pair_ids[:, None], groups[None, :], 0), axis=1)
-    base = jnp.sum(member * before[None, :], axis=1) * GROUP
-    slot = base + rank
-    slot_ids = jnp.arange(slots, dtype=jnp.int32)
-    hot = slot[None, :] == slot_ids[:, None]
-
-    def place(values):
-        return jnp.sum(jnp.where(hot, values[None, :], jnp.zeros_like(values)[None, :]), axis=1)
-
-    return place(weight), place(term_ids), place(source), place(target)
+def arrange(coupling, target, source, live, pairs, slots):
+    terms = target.shape[1]
+    square = (terms, terms)
+
+    def column(row):
+        return jnp.broadcast_to(row, square).T
+
+    def total_of(mask, values):
+        return jnp.sum(jnp.where(mask, values, jnp.zeros_like(values)), axis=0, keepdims=True)
+
+    down = lax.broadcasted_iota(jnp.int32, square, 0)
+    across = lax.broadcasted_iota(jnp.int32, square, 1)
+    ones = jnp.ones(square, jnp.int32)
+    weight = jnp.where(across[:1] < live, coupling, 0.0)
+    target_column = column(target)
+    rank = total_of((target_column == target) & (down < across), ones)
+    base = jnp.zeros_like(target)
+    start = jnp.zeros_like(target)
+    for p in range(pairs):
+        base = jnp.where(target == p, start, base)
+        start = start + ((total_of(target_column == p, ones) + GROUP - 1) & -GROUP)
+    slot = column(base + rank)
+    columns = (column(weight), down, column(source), target_column)
+    placed = []
+    for values in columns:
+        parts = [total_of(slot == across + first, values) for first in range(0, slots, terms)]
+        placed.append(jnp.concatenate(parts, axis=1))
+    return placed
 
 
 def jacobi_kernel(
@@ -66,24 +74,38 @@
     pair_shift_hbm,
     column_margin,
     row_margin,
-    weights_hbm,
-    orders_hbm,
-    sources_hbm,
-    targets_hbm,
+    column_coupling_hbm,
+    row_coupling_hbm,
+    column_target_hbm,
+    row_target_hbm,
+    column_source_hbm,
+    row_source_hbm,
     column_sends_hbm,
     row_sends_hbm,
+    counts_hbm,
     latest_hbm,
     total_hbm,
     amplitudes,
     integrals,
     pno_energy,
+    column_coupling,
+    row_coupling,
+    column_target,
+    row_target,
+    column_source,
+    row_source,
     pair_shift,
+    column_sends,
+    row_sends,
+    counts,
+    arranged_weights,
+    arranged_orders,
+    arranged_sources,
+    arranged_targets,
     weights,
     orders,
     sources,
     targets,
-    column_sends,
-    row_sends,
     margins,
     total,
     frozen,
@@ -98,6 +120,7 @@
     table_in,
     table,
     input_sems,
+    place_sems,
     margin_sems,
     column_send_sems,
     column_recv_sems,
@@ -123,10 +146,13 @@
         (column_sends_hbm, column_sends),
         (row_sends_hbm, row_sends),
         (amplitudes_hbm, amplitudes),
-        (weights_hbm, weights),
-        (orders_hbm, orders),
-        (sources_hbm, sources),
-        (targets_hbm, targets),
+        (counts_hbm, counts),
+        (column_coupling_hbm, column_coupling),
+        (row_coupling_hbm, row_coupling),
+        (column_target_hbm, column_target),
+        (row_target_hbm, row_target),
+        (column_source_hbm, column_source),
+        (row_source_hbm, row_source),
         (pair_shift_hbm, pair_shift),
         (pno_energy_hbm, pno_energy),
         (integrals_hbm, integrals),
@@ -346,10 +372,37 @@
 
     for sweep in range(ITERS):
         launch(sweep)
+        if sweep == 0:
+            for copy in stage_copies[3:10]:
+                copy.wait()
+            terms_in = (
+                (column_coupling, column_target, column_source),
+                (row_coupling, row_target, row_source),
+            )
+            staging = (arranged_weights, arranged_orders, arranged_sources, arranged_targets)
+            for side in range(2):
+                coupling, target, source = terms_in[side]
+                rows = arrange(
+                    coupling[...],
+                    target[...],
+                    source[...],
+                    counts[0, side],
+                    pairs,
+                    weights.shape[1],
+                )
+                for stage, row in zip(staging, rows):
+                    stage[side : side + 1, :] = row
+            settled = (weights, orders, sources, targets)
+            placements = [
+                pltpu.make_async_copy(stage, settled[i], place_sems.at[i])
+                for i, stage in enumerate(staging)
+            ]
+            for copy in placements:
+                copy.start()
         pass_on(sweep)
         total[...] = jnp.zeros_like(total)
         if sweep == 0:
-            for copy in stage_copies[3:]:
+            for copy in stage_copies[10:] + placements:
                 copy.wait()
             for side in range(2):
                 for chunk in range(chunks):
@@ -380,20 +433,17 @@
 
 
 def shards(sizes, *operands):
-    counts = operands[14]
-    pairs = operands[0].shape[0]
-    couplings, targets, sources = (jnp.stack(operands[i : i + 2]) for i in (6, 8, 10))
-    arranged = jax.vmap(functools.partial(arrange, pairs=pairs))(
-        couplings, targets, sources, counts[0]
-    )
-    operands = operands[:6] + arranged + (operands[12].T, operands[13].T)
+    lists = tuple(values.reshape(1, -1) for values in operands[6:12])
+    operands = operands[:6] + lists + (operands[12].T, operands[13].T, operands[14])
     amplitudes, pno_energy, column_margin = operands[0], operands[2], operands[4]
-    column_sends = operands[10]
+    column_sends = operands[12]
     terms, width, _ = column_margin.shape
     cap = column_sends.shape[0]
+    slots = -(-slot_count(terms, amplitudes.shape[0]) // terms) * terms
+    listed = [(2, slots, jnp.float32)] + [(2, slots, jnp.int32)] * 3
     hbm = pl.BlockSpec(memory_space=pltpu.HBM)
-    in_vmem = (0, 1, 2)
-    in_smem = (3,) + tuple(range(6, 12))
+    in_vmem = (0, 1, 2) + tuple(range(6, 12))
+    in_smem = (3, 12, 13, 14)
 
     def held(i, space):
         return space(operands[i].shape, operands[i].dtype)
@@ -409,6 +459,7 @@
             out_specs=[hbm] * 2,
             scratch_shapes=[held(i, pltpu.VMEM) for i in in_vmem]
             + [held(i, pltpu.SMEM) for i in in_smem]
+            + [space((n, m), kind) for space in (pltpu.VMEM, pltpu.SMEM) for n, m, kind in listed]
             + [
                 buffer(2, terms),
                 pltpu.VMEM(amplitudes.shape, jnp.float32),
@@ -419,11 +470,12 @@
             + [buffer(size * cap) for size in sizes] * ITERS
             + [buffer(amplitudes.shape[0])] * ITERS
             + [
-                held(11, pltpu.VMEM),
-                held(11, pltpu.SMEM),
+                held(13, pltpu.VMEM),
+                held(13, pltpu.SMEM),
             ]
             + [
                 dma((len(in_vmem) + len(in_smem),)),
+                dma((len(listed),)),
                 dma((2, terms // CHUNK)),
                 dma((ITERS, sizes[0])),
                 dma((ITERS, sizes[0])),

time: 41.3 us -> 37.7 us (0.913)
  other arithmetic: 5.65 us -> 1.97 us
    reduce_sum x6 -> x0, other arithmetic: 2.17 us -> none  [the longest x2 1.61 us: place(): jnp.sum(jnp.where(hot, values[None, :], jnp.zeros_like(values)[None, :]),...]
    select_n x2 -> x0, other arithmetic: 0.77 us -> none  [the longest x1 0.76 us: arrange(): weight = jnp.where(term_ids < live, coupling, 0.0)]
    another operation x1 -> x0, other arithmetic: 0.71 us -> none  [shards(): jnp.stack(operands[i:i + 2])]
where the time goes in v3:
time: 37.7 us; the launch traced here: 37.6 us
  Pallas kernels  34.9 us (93%)
  other arithmetic  1.97 us (5%)
  between operations  0.69 us (2%)
    pallas_call x1, Pallas kernels, shards(): pl.pallas_call(functools.partial(jacobi_kernel, sizes), out_shape=[jax.Sh...  34.9 us
    sub x1, other arithmetic, shards(): return (latest - residual / divisor, residual)  1.97 us

profile of v3, /device:TPU:0, one launch (start us, length us, event | category | flops | bytes accessed | tf_op | source)
XLA Modules:
  0.0 37.6 jit_solution(4151409655196411480)
XLA Ops:
  0.6 0.0 copy-start
  0.6 0.0 copy-start.1
  0.7 0.0 copy-start.2
  0.7 34.9 %jacobi.1 = (f32[4,128,128]{2,1,0:T(8,128)}, f32[4,128,128]{2,1,0:T(8,128)}) custom-call(f32[4,128,128]{2,1,0:T(8,128)} %amplitudes_hbm.1, f32[4,128,128]{2,1,0:T(8,128)} %integrals_hbm.1, f32[4,128]{1,0:T(4,128)} %pno_energy_hbm.1, f32[4]{0:T(128)} %pair_shift_hbm.1, bf16[128,128,128]{2,1,0:T(8,128)(2,1)} %column_margin.1, ...), custom_call_target="tpu_custom_call" | custom-call | tf_op jit(solution)/shard_map/jacobi/pallas_call | solution.py:455
  35.6 0.0 copy-done
  35.6 0.0 copy-done.1
  35.6 0.0 copy-done.2
  35.6 2.0 %divide_subtract_fusion = (f32[4,128,128]{2,1,0:T(8,128)}, f32[4,128,128]{2,1,0:T(8,128)}) fusion(f32[4,128,128]{2,1,0:T(8,128)} %get-tuple-element.4, f32[4]{0:T(128)S(1)} %copy-done.2, f32[4,128]{1,0:T(4,128)S(1)} %copy-done.1, f32[4,128,128]{2,1,0:T(8,128)} %get-tuple-element.5, f32[4,128,128]{2,1,0:T(8,128)S(1)} %copy-done), kind=kLoop, calls=%fused_computation | loop fusion | flops 458752 | bytes 1312784 | tf_op jit(solution)/shard_map/sub | solution.py:497
Async XLA Ops:
  0.6 35.0 %copy-start = (f32[4,128,128]{2,1,0:T(8,128)S(1)}, f32[4,128,128]{2,1,0:T(8,128)}, u32[]{:S(2)}) copy-start(f32[4,128,128]{2,1,0:T(8,128)} %integrals_hbm.1) | copy-start | bytes 786436
  0.6 35.0 %copy-start.1 = (f32[4,128]{1,0:T(4,128)S(1)}, f32[4,128]{1,0:T(4,128)}, u32[]{:S(2)}) copy-start(f32[4,128]{1,0:T(4,128)} %pno_energy_hbm.1) | copy-start | bytes 6148
  0.7 35.0 %copy-start.2 = (f32[4]{0:T(128)S(1)}, f32[4]{0:T(128)}, u32[]{:S(2)}) copy-start(f32[4]{0:T(128)} %pair_shift_hbm.1) | copy-start | bytes 52
